TPU v7x, 32 devices: a whole 2x2x4 slice. The times are simulated.
32 devices in a mesh: expert: 8 (over z, x), chan: 4 (over y, core).
Axes of the slice: x: 2, y: 2, z: 4, core: 2. Of those that a mesh axis runs over, the one named last changes fastest.
Arguments:
- rows_in: bfloat16 [256, 6144], P('expert', 'chan'), may hold values from -6 to 6
- expert_picks: int32 [256, 2], P('expert'), may hold values from 0 to 3, all different within a row; in each aligned block of 32 rows (0 to 31, 32 to 63, ...) at most 18 rows name the same one
- latent_ids: int32 [256, 2, 32], P('expert'), may hold values from 0 to 8191, as said below
- enc_weight: bfloat16 [6144, 32768], P('chan', 'expert'), may hold values from -0.078125 to 0.078125
- dec_weight: bfloat16 [32768, 6144], P('expert', 'chan'), may hold values from -0.375 to 0.375
Outputs:
- recon_error: bfloat16 [256, 6144], P('expert', 'chan')
- enc_grad: float32 [6144, 32768], P('chan', 'expert')
- dec_grad: float32 [32768, 6144], P('expert', 'chan')
Inputs may be any that keep to these rules, and one draw needn't show every extreme that they name: `expert_picks`: A row's two experts differ; among the 32 rows of one device at most 18 name one expert. latent_ids[r, j, k] lies in k * 256 to (k + 1) * 256 - 1 and numbers a latent of expert expert_picks[r, j].
All inputs are finite; a program needn't handle non-finite values.
Results may differ from a plain program's by a relative error of at most 0.0095.
Values may be sent and summed in bfloat16 or wider, within the bound.
No kernel may reach another device: no remote copies, remote signals or barrier semaphores. Data moves between devices by JAX's collectives and lax.ppermute only.
A program may use at most 128 MiB of HBM per device.

v0:
```python
import jax
import jax.numpy as jnp
from jax import lax
from jax.sharding import PartitionSpec as P

LAT = 8192
EXPERTS = 4
TOPK = 32
CAP = 18


def latent_mask(chosen, lat_low, lat_local):
    stride = LAT // TOPK
    id_block = lax.dynamic_slice_in_dim(chosen, lat_low // stride, lat_local // stride, 1)
    spread = jnp.repeat(id_block, stride, axis=1)
    return spread == (lat_low + lax.iota(jnp.int32, lat_local))[None, :]


def encode(flat_rows, chosen, enc_weight, lat_low):
    lat_local = enc_weight.shape[1]
    live_mask = latent_mask(chosen, lat_low, lat_local)
    partial_pre = jnp.dot(flat_rows, enc_weight, preferred_element_type=jnp.float32)
    preact = lax.psum(partial_pre, "chan")
    activation = jnp.where(live_mask, preact, 0.0).astype(jnp.bfloat16)
    return (live_mask, activation)


def gradients(flat_rows, flat_errors, live_mask, activation, dec_weight):
    partial_grad = lax.dot_general(
        flat_errors, dec_weight, (((1,), (1,)), ((), ())), preferred_element_type=jnp.float32
    )
    act_grad = lax.psum(partial_grad.astype(jnp.bfloat16), "chan").astype(jnp.float32)
    pre_grad = jnp.where(live_mask, act_grad, 0.0).astype(jnp.bfloat16)
    dec_grad = lax.dot_general(
        activation, flat_errors, (((0,), (0,)), ((), ())), preferred_element_type=jnp.float32
    )
    enc_grad = lax.dot_general(
        flat_rows, pre_grad, (((0,), (0,)), ((), ())), preferred_element_type=jnp.float32
    )
    return (enc_grad, dec_grad)


def per_device(rows_in, expert_picks, latent_ids, enc_weight, dec_weight):
    row_count, chan_width = rows_in.shape
    devices = lax.axis_size("expert")
    group_size = devices // EXPERTS
    lat_local = enc_weight.shape[1]
    position = lax.axis_index("expert")
    lat_low = position % group_size * lat_local
    capacity = CAP
    hit_table = (expert_picks[:, :, None] == lax.iota(jnp.int32, EXPERTS)[None, None, :]).astype(
        jnp.int32
    )
    member = jnp.sum(hit_table, axis=1)
    earlier = (
        lax.iota(jnp.int32, row_count)[None, :] < lax.iota(jnp.int32, row_count)[:, None]
    ).astype(jnp.int32)
    slot_index = jnp.dot(earlier, member)
    slot_table = (slot_index[:, :, None] == lax.iota(jnp.int32, capacity)[None, None, :]) & (
        member[:, :, None] > 0
    )
    slot_bf = slot_table.astype(jnp.bfloat16)
    picked_ids = jnp.einsum("rje,rjk->rek", hit_table, latent_ids + 1)
    sent_rows = jnp.einsum(
        "rec,rd->ecd", slot_bf, rows_in, preferred_element_type=jnp.float32
    ).astype(jnp.bfloat16)
    sent_ids = jnp.einsum("rec,rek->eck", slot_table.astype(jnp.int32), picked_ids) - 1

    def fan_out(table):
        wide = jnp.broadcast_to(table[:, None], (EXPERTS, group_size) + table.shape[1:])
        return wide.reshape((devices,) + table.shape[1:])

    got_rows, got_ids = (
        lax.all_to_all(fan_out(sent_rows), "expert", split_axis=0, concat_axis=0, tiled=True),
        lax.all_to_all(fan_out(sent_ids), "expert", split_axis=0, concat_axis=0, tiled=True),
    )
    flat_rows = got_rows.reshape(devices * capacity, chan_width)
    chosen = got_ids.reshape(devices * capacity, TOPK)
    live_mask, activation = encode(flat_rows, chosen, enc_weight, lat_low)
    partial_recon = jnp.dot(activation, dec_weight, preferred_element_type=jnp.float32)
    returned = lax.all_to_all(
        partial_recon.reshape(devices, capacity, chan_width).astype(jnp.bfloat16),
        "expert",
        split_axis=0,
        concat_axis=0,
        tiled=True,
    ).astype(jnp.float32)
    per_expert = jnp.sum(returned.reshape(EXPERTS, group_size, capacity, chan_width), axis=1)
    recon = jnp.einsum(
        "rec,ecd->rd", slot_table.astype(jnp.float32), per_expert, precision=lax.Precision.HIGHEST
    )
    recon_error = (recon - rows_in.astype(jnp.float32)).astype(jnp.bfloat16)
    sent_errors = jnp.einsum(
        "rec,rd->ecd", slot_bf, recon_error, preferred_element_type=jnp.float32
    ).astype(jnp.bfloat16)
    got_errors = lax.all_to_all(
        fan_out(sent_errors), "expert", split_axis=0, concat_axis=0, tiled=True
    )
    flat_errors = got_errors.reshape(devices * capacity, chan_width)
    enc_grad, dec_grad = gradients(flat_rows, flat_errors, live_mask, activation, dec_weight)
    return (recon_error, enc_grad, dec_grad)


def solution(mesh):
    placed = (
        P("expert", "chan"),
        P("expert", None),
        P("expert", None, None),
        P("chan", "expert"),
        P("expert", "chan"),
    )
    return jax.shard_map(
        per_device,
        mesh=mesh,
        in_specs=placed,
        out_specs=(P("expert", "chan"), P("chan", "expert"), P("expert", "chan")),
        check_vma=False,
    )
```

profile of v0, /device:TPU:0, one launch (start us, length us, event | category | flops | bytes accessed | tf_op | source)
XLA Modules:
  0.0 208.2 jit_solution(4997542280732348640)
XLA Ops:
  7.2 0.8 copy.21
  7.9 0.1 convert_reduce_fusion.1
  8.1 0.2 fusion.25
  8.3 1.3 fusion.13
  9.6 0.2 convolution_add_fusion
  9.8 0.7 reshape.63
  10.5 7.3 %all-to-all-start = ((s32[8,1,576]{2,1,0:T(1,128)}), s32[8,1,576]{2,1,0:T(1,128)S(1)}, u32[]{:S(2)}, u32[]{:S(2)}) async-start(s32[8,1,576]{2,1,0:T(1,128)} %reshape.63), calls=%async_computation | async-start | bytes 40960 | tf_op jit(solution)/shard_map/all_to_all | solution.py:75
  17.8 1.1 convolution_convert_fusion.3
  19.0 5.4 %all-to-all-done = s32[8,1,576]{2,1,0:T(1,128)S(1)} async-done(((s32[8,1,576]{2,1,0:T(1,128)}), s32[8,1,576]{2,1,0:T(1,128)S(1)}, u32[]{:S(2)}, u32[]{:S(2)}) %all-to-all-start) | async-done | bytes 18464 | tf_op jit(solution)/shard_map/all_to_all | solution.py:75
  24.4 0.9 broadcast_in_dim.14
  25.3 3.5 %all-to-all-start.1 = ((bf16[8,18,1536]{2,1,0:T(8,128)(2,1)}), bf16[8,18,1536]{2,1,0:T(8,128)(2,1)S(1)}, u32[]{:S(2)}, u32[]{:S(2)}) async-start(bf16[8,18,1536]{2,1,0:T(8,128)(2,1)} %bitcast.2), calls=%async_computation.1 | async-start | bytes 1179648 | tf_op jit(solution)/shard_map/all_to_all | solution.py:74
  28.9 0.5 broadcast.21
  29.4 0.7 reduce
  30.3 0.4 broadcast_in_dim.13
  30.6 1.9 copy.28
  32.6 0.4 broadcast_compare_fusion
  32.9 10.5 %all-to-all-done.1 = bf16[8,18,1536]{2,1,0:T(8,128)(2,1)S(1)} async-done(((bf16[8,18,1536]{2,1,0:T(8,128)(2,1)}), bf16[8,18,1536]{2,1,0:T(8,128)(2,1)S(1)}, u32[]{:S(2)}, u32[]{:S(2)}) %all-to-all-start.1) | async-done | bytes 442400 | tf_op jit(solution)/shard_map/all_to_all | solution.py:74
  43.5 0.1 reshape.52
  43.6 6.6 %fusion.30 = f32[144,4096]{1,0:T(8,128)S(1)} fusion(bf16[144,1536]{1,0:T(8,128)(2,1)S(1)} %reshape.52, bf16[1536,4096]{1,0:T(8,128)(2,1)} %param.8), kind=kOutput, calls=%fused_computation.43 | convolution fusion | flops 1811939328 | bytes 15384576 | tf_op jit(solution)/shard_map/dot_general | solution.py:22
  50.2 45.4 %all-reduce.4 = bf16[144,4096]{1,0:T(8,128)(2,1)} all-reduce(f32[144,4096]{1,0:T(8,128)S(1)} %fusion.30), channel_id=1, replica_groups=mesh['expert'=8,'chan'=4] {'chan'}, use_global_device_ids=true, to_apply=%region_1.2 | all-reduce | flops 589824 | bytes 3538944 | tf_op jit(solution)/shard_map/psum | solution.py:23
  95.6 7.0 %convolution_convert_fusion.1 = bf16[144,1536]{1,0:T(8,128)(2,1)S(1)} fusion(bf16[4096,1536]{1,0:T(8,128)(2,1)} %param.9, pred[144,4096]{1,0:T(8,128)(4,1)S(1)} %broadcast_compare_fusion, bf16[144,4096]{1,0:T(8,128)(2,1)} %all-reduce.4), kind=kOutput, calls=%fused_computation.1 | convolution fusion | flops 1812750336 | bytes 14794752 | tf_op jit(solution)/shard_map/dot_general | solution.py:80
  102.6 0.1 convert_element_type.42
  102.7 20.3 %all_to_all.20 = bf16[8,18,1536]{2,1,0:T(8,128)(2,1)S(1)} all-to-all(bf16[8,18,1536]{2,1,0:T(8,128)(2,1)S(1)} %convert_element_type.42), channel_id=1, replica_groups=mesh['expert'=8,'chan'=4] {'expert'}, dimensions={0} | all-to-all | bytes 884736 | tf_op jit(solution)/shard_map/all_to_all | solution.py:81
  123.0 0.1 convert_reduce_fusion
  123.1 0.3 fusion.1
  123.5 0.2 convolution_convert_fusion.2
  123.7 19.3 %all_to_all.21 = bf16[8,18,1536]{2,1,0:T(8,128)(2,1)S(1)} all-to-all(bf16[8,18,1536]{2,1,0:T(8,128)(2,1)S(1)} %bitcast.31), channel_id=1, replica_groups=mesh['expert'=8,'chan'=4] {'expert'}, dimensions={0} | all-to-all | bytes 884736 | tf_op jit(solution)/shard_map/all_to_all | solution.py:96
  143.0 0.1 reshape.56
  143.2 9.9 %convolution_convert_fusion = bf16[144,4096]{1,0:T(8,128)(2,1)} fusion(bf16[144,1536]{1,0:T(8,128)(2,1)S(1)} %reshape.56, bf16[4096,1536]{1,0:T(8,128)(2,1)} %param.9), kind=kOutput, calls=%fused_computation | convolution fusion | flops 1812529152 | bytes 14204928 | tf_op jit(solution)/shard_map/dot_general | solution.py:29
  153.1 10.8 %fusion.4 = f32[4096,1536]{1,0:T(8,128)} fusion(bf16[144,1536]{1,0:T(8,128)(2,1)S(1)} %reshape.56, pred[144,4096]{1,0:T(8,128)(4,1)S(1)} %broadcast_compare_fusion, bf16[144,4096]{1,0:T(8,128)(2,1)S(1)} %copy-done), kind=kOutput, calls=%fused_computation.14 | convolution fusion | flops 1812529152 | bytes 27377664 | tf_op jit(solution)/shard_map/dot_general | solution.py:34
  163.9 25.4 %all-reduce.3.cloned.1.call-done = bf16[144,4096]{1,0:T(8,128)(2,1)} async-done(((bf16[144,4096]{1,0:T(8,128)(2,1)}), bf16[144,4096]{1,0:T(8,128)(2,1)}) %all-reduce.3.cloned.1.call-update) | async-done | bytes 1179664 | tf_op jit(solution)/shard_map/psum | solution.py:32
  189.3 12.0 %fusion.2 = f32[1536,4096]{1,0:T(8,128)} fusion(bf16[144,1536]{1,0:T(8,128)(2,1)S(1)} %reshape.52, pred[144,4096]{1,0:T(8,128)(4,1)S(1)} %broadcast_compare_fusion, bf16[144,4096]{1,0:T(8,128)(2,1)} %all-reduce.3.cloned.1.call-done), kind=kOutput, calls=%fused_computation.9 | convolution fusion | flops 1813708800 | bytes 27377664 | tf_op jit(solution)/shard_map/dot_general | solution.py:37
  (16 shorter events, 0.4 us)
Async XLA Ops:
  10.5 13.9 %all-to-all-start = ((s32[8,1,576]{2,1,0:T(1,128)}), s32[8,1,576]{2,1,0:T(1,128)S(1)}, u32[]{:S(2)}, u32[]{:S(2)}) async-start(s32[8,1,576]{2,1,0:T(1,128)} %reshape.63), calls=%async_computation | async-start | bytes 40960 | tf_op jit(solution)/shard_map/all_to_all | solution.py:75
  25.3 18.2 %all-to-all-start.1 = ((bf16[8,18,1536]{2,1,0:T(8,128)(2,1)}), bf16[8,18,1536]{2,1,0:T(8,128)(2,1)S(1)}, u32[]{:S(2)}, u32[]{:S(2)}) async-start(bf16[8,18,1536]{2,1,0:T(8,128)(2,1)} %bitcast.2), calls=%async_computation.1 | async-start | bytes 1179648 | tf_op jit(solution)/shard_map/all_to_all | solution.py:74
  28.8 160.5 %all-reduce.3.cloned.1.call-start = ((), (), s32[]{:S(2)}) async-start(), calls=%async_computation.4 | async-start | bytes 2359296 | tf_op jit(solution)/shard_map/psum | solution.py:32
  102.6 20.5 %copy-start.1 = (bf16[32,1536]{1,0:T(8,128)(2,1)S(1)}, bf16[32,1536]{1,0:T(8,128)(2,1)}, u32[]{:S(2)}) copy-start(bf16[32,1536]{1,0:T(8,128)(2,1)} %param.5) | copy-start | bytes 294916
  123.4 29.6 %copy-start.2 = (bf16[32,1536]{1,0:T(8,128)(2,1)}, bf16[32,1536]{1,0:T(8,128)(2,1)S(1)}, u32[]{:S(2)}) copy-start(bf16[32,1536]{1,0:T(8,128)(2,1)S(1)} %fusion.1) | copy-start | bytes 294916
  143.2 9.9 %copy-start = (bf16[144,4096]{1,0:T(8,128)(2,1)S(1)}, bf16[144,4096]{1,0:T(8,128)(2,1)}, u32[]{:S(2)}) copy-start(bf16[144,4096]{1,0:T(8,128)(2,1)} %all-reduce.4) | copy-start | bytes 3538948
Sparse Core Ops, SparseCore 0:
  153.2 36.1 all-reduce.2
where the time goes:
time: 209 us; the launch traced here: 208 us
  blocking collectives  85 us (41%)
  matrix products  49.6 us (24%)
  waiting for transfers between devices  41.4 us (20%)
  between operations  14.3 us (7%)
  starting transfers between devices  10.9 us (5%)
  local copies, waits for them, and re-layouts  5.84 us (3%)
    psum x1, blocking collectives, encode(): preact = lax.psum(partial_pre, 'chan')  45.4 us
    psum x1, waiting for transfers between devices, gradients(): lax.psum(partial_grad.astype(jnp.bfloat16), 'chan').astype(jnp.float32)  25.4 us
    all_to_all x1, blocking collectives, per_device(): lax.all_to_all(partial_recon.reshape(devices, capacity, chan_width).astyp...  20.3 us
    all_to_all x1, blocking collectives, per_device(): lax.all_to_all(fan_out(sent_errors), 'expert', split_axis=0, concat_axis=...  19.3 us
    dot_general x1, matrix products, gradients(): lax.dot_general(flat_rows, pre_grad, (((0,), (0,)), ((), ())), preferred_...  12 us
    dot_general x1, matrix products, gradients(): lax.dot_general(activation, flat_errors, (((0,), (0,)), ((), ())), prefer...  10.8 us
    all_to_all x1, waiting for transfers between devices, per_device(): lax.all_to_all(fan_out(sent_rows), 'expert', split_axis=0, concat_axis=0,...  10.5 us
    dot_general x1, matrix products, gradients(): lax.dot_general(flat_errors, dec_weight, (((1,), (1,)), ((), ())), prefer...  9.88 us
  transfers between devices with their start and end apart: 3, of which 3 were waited for; matrix products, arithmetic and copies ran while one was open for 8% of the time, Pallas kernels for 0%

commit v1 on v0

--- a/solution.py
+++ b/solution.py
@@ -9,28 +9,41 @@
 CAP = 18
 
 
-def latent_mask(chosen, lat_low, lat_local):
-    stride = LAT // TOPK
-    id_block = lax.dynamic_slice_in_dim(chosen, lat_low // stride, lat_local // stride, 1)
-    spread = jnp.repeat(id_block, stride, axis=1)
-    return spread == (lat_low + lax.iota(jnp.int32, lat_local))[None, :]
+def spread(values, places, stride):
+    ids = lax.iota(jnp.int32, stride)
+    hit = places[:, :, None] == ids[None, None, :]
+    table = jnp.where(hit, values[:, :, None], 0.0).astype(jnp.bfloat16)
+    return table.reshape(values.shape[0], values.shape[1] * stride)
 
 
-def encode(flat_rows, chosen, enc_weight, lat_low):
-    lat_local = enc_weight.shape[1]
-    live_mask = latent_mask(chosen, lat_low, lat_local)
-    partial_pre = jnp.dot(flat_rows, enc_weight, preferred_element_type=jnp.float32)
-    preact = lax.psum(partial_pre, "chan")
-    activation = jnp.where(live_mask, preact, 0.0).astype(jnp.bfloat16)
-    return (live_mask, activation)
+def gather_live(partial, places, stride):
+    ids = lax.iota(jnp.int32, stride)
+    hit = places[:, :, None] == ids[None, None, :]
+    return jnp.sum(jnp.where(hit, partial.reshape(hit.shape), 0.0), axis=2)
 
 
-def gradients(flat_rows, flat_errors, live_mask, activation, dec_weight):
+def live_places(chosen, lat_low, lat_local):
+    stride = LAT // TOPK
+    first = lat_low // stride
+    count = lat_local // stride
+    id_block = lax.dynamic_slice_in_dim(chosen, first, count, 1)
+    return id_block - (first + lax.iota(jnp.int32, count))[None, :] * stride
+
+
+def encode(flat_rows, places, enc_weight):
+    stride = LAT // TOPK
+    partial_pre = jnp.dot(flat_rows, enc_weight, preferred_element_type=jnp.float32)
+    live = lax.psum(gather_live(partial_pre, places, stride), "chan")
+    return spread(live, places, stride)
+
+
+def gradients(flat_rows, flat_errors, places, activation, dec_weight):
+    stride = LAT // TOPK
     partial_grad = lax.dot_general(
         flat_errors, dec_weight, (((1,), (1,)), ((), ())), preferred_element_type=jnp.float32
     )
-    act_grad = lax.psum(partial_grad.astype(jnp.bfloat16), "chan").astype(jnp.float32)
-    pre_grad = jnp.where(live_mask, act_grad, 0.0).astype(jnp.bfloat16)
+    live = lax.psum(gather_live(partial_grad, places, stride), "chan")
+    pre_grad = spread(live, places, stride)
     dec_grad = lax.dot_general(
         activation, flat_errors, (((0,), (0,)), ((), ())), preferred_element_type=jnp.float32
     )
@@ -76,7 +89,8 @@
     )
     flat_rows = got_rows.reshape(devices * capacity, chan_width)
     chosen = got_ids.reshape(devices * capacity, TOPK)
-    live_mask, activation = encode(flat_rows, chosen, enc_weight, lat_low)
+    places = live_places(chosen, lat_low, lat_local)
+    activation = encode(flat_rows, places, enc_weight)
     partial_recon = jnp.dot(activation, dec_weight, preferred_element_type=jnp.float32)
     returned = lax.all_to_all(
         partial_recon.reshape(devices, capacity, chan_width).astype(jnp.bfloat16),
@@ -97,7 +111,7 @@
         fan_out(sent_errors), "expert", split_axis=0, concat_axis=0, tiled=True
     )
     flat_errors = got_errors.reshape(devices * capacity, chan_width)
-    enc_grad, dec_grad = gradients(flat_rows, flat_errors, live_mask, activation, dec_weight)
+    enc_grad, dec_grad = gradients(flat_rows, flat_errors, places, activation, dec_weight)
     return (recon_error, enc_grad, dec_grad)
 
 

time: 209 us -> 157 us (0.75)
  blocking collectives: 85 us -> 42.4 us
  waiting for transfers between devices: 41.4 us -> 20.3 us
  local copies, waits for them, and re-layouts: 5.84 us -> 25 us
  between operations: 14.3 us -> 0.9 us
  starting transfers between devices: 10.9 us -> 14.4 us
    psum x1 -> x0, waiting for transfers between devices: 25.4 us -> none  [gradients(): lax.psum(partial_grad.astype(jnp.bfloat16), 'chan').astype(jnp.float32)]
    psum x1 -> x2, blocking collectives: 45.4 us -> 20.5 us  [the longest x1 10.3 us: gradients(): live = lax.psum(gather_live(partial_grad, places, stride), 'chan')]
    all_to_all x1 -> x0, blocking collectives: 19.3 us -> none  [per_device(): lax.all_to_all(fan_out(sent_errors), 'expert', split_axis=0, concat_axis=...]
    dot_general x0 -> x1, local copies, waits for them, and re-layouts: none -> 16.6 us  [encode(): jnp.dot(flat_rows, enc_weight, preferred_element_type=jnp.float32)]
    all_to_all x0 -> x1, waiting for transfers between devices: none -> 14.8 us  [per_device(): lax.all_to_all(fan_out(sent_errors), 'expert', split_axis=0, concat_axis=...]
    all_to_all x1, waiting for transfers between devices: 10.5 us -> 0.01 us  [per_device(): lax.all_to_all(fan_out(sent_rows), 'expert', split_axis=0, concat_axis=0,...]
    all_to_all x0 -> x1, starting transfers between devices: none -> 3.54 us  [per_device(): lax.all_to_all(fan_out(sent_errors), 'expert', split_axis=0, concat_axis=...]
    dot_general x1, matrix products: 6.58 us -> 8.99 us  [encode(): jnp.dot(flat_rows, enc_weight, preferred_element_type=jnp.float32)]
  transfers between devices with their start and end apart: 3 -> 3, of which waited for: 3 -> 2; matrix products, arithmetic and copies ran while one was open for 8% -> 14% of each run, Pallas kernels for 0% -> 0%
where the time goes in v1:
time: 157 us; the launch traced here: 156 us
  matrix products  51.2 us (33%)
  blocking collectives  42.4 us (27%)
  local copies, waits for them, and re-layouts  25 us (16%)
  waiting for transfers between devices  20.3 us (13%)
  starting transfers between devices  14.4 us (9%)
  other arithmetic  2.22 us (1%)
    all_to_all x1, blocking collectives, per_device(): lax.all_to_all(partial_recon.reshape(devices, capacity, chan_width).astyp...  22 us
    dot_general x1, local copies, waits for them, and re-layouts, encode(): jnp.dot(flat_rows, enc_weight, preferred_element_type=jnp.float32)  16.6 us
    all_to_all x1, waiting for transfers between devices, per_device(): lax.all_to_all(fan_out(sent_errors), 'expert', split_axis=0, concat_axis=...  14.8 us
    dot_general x1, matrix products, gradients(): lax.dot_general(activation, flat_errors, (((0,), (0,)), ((), ())), prefer...  10.8 us
    dot_general x1, matrix products, gradients(): lax.dot_general(flat_rows, pre_grad, (((0,), (0,)), ((), ())), preferred_...  10.8 us
    psum x1, blocking collectives, gradients(): live = lax.psum(gather_live(partial_grad, places, stride), 'chan')  10.3 us
    psum x1, blocking collectives, encode(): live = lax.psum(gather_live(partial_pre, places, stride), 'chan')  10.1 us
    dot_general x1, matrix products, encode(): jnp.dot(flat_rows, enc_weight, preferred_element_type=jnp.float32)  8.99 us
  transfers between devices with their start and end apart: 3, of which 2 were waited for; matrix products, arithmetic and copies ran while one was open for 14% of the time, Pallas kernels for 0%

profile of v1, /device:TPU:0, one launch (start us, length us, event | category | flops | bytes accessed | tf_op | source)
XLA Modules:
  0.0 156.4 jit_solution(1998265762523869602)
XLA Ops:
  0.6 0.8 copy.35
  1.5 0.2 fusion.31
  1.8 1.3 fusion.19
  3.1 0.2 convolution_add_fusion
  3.3 0.7 reshape.154
  4.0 7.3 %all-to-all-start = ((s32[8,1,576]{2,1,0:T(1,128)}), s32[8,1,576]{2,1,0:T(1,128)S(1)}, u32[]{:S(2)}, u32[]{:S(2)}) async-start(s32[8,1,576]{2,1,0:T(1,128)} %reshape.154), calls=%async_computation | async-start | bytes 40960 | tf_op jit(solution)/shard_map/all_to_all | solution.py:88
  11.3 1.1 convolution_convert_fusion.1
  12.4 5.5 %all-to-all-done = s32[8,1,576]{2,1,0:T(1,128)S(1)} async-done(((s32[8,1,576]{2,1,0:T(1,128)}), s32[8,1,576]{2,1,0:T(1,128)S(1)}, u32[]{:S(2)}, u32[]{:S(2)}) %all-to-all-start) | async-done | bytes 18464 | tf_op jit(solution)/shard_map/all_to_all | solution.py:88
  17.9 0.9 broadcast_in_dim.32
  18.7 3.5 %all-to-all-start.1 = ((bf16[8,18,1536]{2,1,0:T(8,128)(2,1)}), bf16[8,18,1536]{2,1,0:T(8,128)(2,1)S(1)}, u32[]{:S(2)}, u32[]{:S(2)}) async-start(bf16[8,18,1536]{2,1,0:T(8,128)(2,1)} %bitcast.2), calls=%async_computation.1 | async-start | bytes 1179648 | tf_op jit(solution)/shard_map/all_to_all | solution.py:87
  22.3 16.6 %copy.45 = bf16[4096,1536]{1,0:T(8,128)(2,1)} copy(bf16[4096,1536]{0,1:T(8,128)(2,1)} %bitcast.45) | data formatting | bytes 25165824 | tf_op jit(solution)/shard_map/dot_general | solution.py:35
  38.9 0.5 broadcast.117
  39.4 0.7 reduce
  40.6 0.4 eq.95.clone
  41.0 1.9 %eq.96 = s32[8,18,4096]{2,1,0:T(8,128)} reshape(s32[144,16,256]{2,1,0:T(8,128)S(1)} %eq.95.clone) | data formatting | bytes 4718592 | tf_op jit(solution)/shard_map/eq | solution.py:14
  43.0 9.0 %select_reduce_fusion.1 = f32[144,16]{0,1:T(8,128)S(1)} fusion(bf16[144,1536,1]{1,0,2:T(8,128)(2,1)S(1)} %reshape.146, bf16[16,256,1536]{2,1,0:T(8,128)(2,1)} %bitcast.46, s32[144,16]{0,1:T(8,128)S(1)} %broadcast_subtract_fusion), kind=kOutput, calls=%fused_computation.7 | convolution fusion | flops 1813706496 | bytes 13043712 | tf_op jit(solution)/shard_map/dot_general | solution.py:35
  52.0 10.1 %psum.14 = bf16[144,16]{0,1:T(8,128)(2,1)S(1)} all-reduce(f32[144,16]{0,1:T(8,128)S(1)} %select_reduce_fusion.1), channel_id=1, replica_groups=mesh['expert'=8,'chan'=4] {'chan'}, use_global_device_ids=true, to_apply=%region_2.3 | all-reduce | flops 2304 | bytes 13824 | tf_op jit(solution)/shard_map/psum | solution.py:36
  62.3 0.4 broadcast_in_dim.34.clone
  62.6 0.7 broadcast_in_dim.35
  63.3 8.4 %fusion.2 = bf16[8,18,1536]{2,1,0:T(8,128)(2,1)S(1)} fusion(bf16[4096,1536]{1,0:T(8,128)(2,1)} %param.9, bf16[8,18,4096]{2,1,0:T(8,128)(2,1)S(1)} %broadcast_in_dim.35, s32[8,18,4096]{2,1,0:T(8,128)} %eq.96, s32[4096]{0:T(1024)S(1)} %bitcast.50), kind=kOutput, calls=%fused_computation.3 | convolution fusion | flops 1813340160 | bytes 16580608 | tf_op jit(solution)/shard_map/dot_general | solution.py:94
  71.7 22.0 %all_to_all.20 = bf16[8,18,1536]{2,1,0:T(8,128)(2,1)S(1)} all-to-all(bf16[8,18,1536]{2,1,0:T(8,128)(2,1)S(1)} %fusion.2), channel_id=1, replica_groups=mesh['expert'=8,'chan'=4] {'expert'}, dimensions={0} | all-to-all | bytes 884736 | tf_op jit(solution)/shard_map/all_to_all | solution.py:95
  93.9 0.3 fusion.6
  94.2 0.2 convolution_convert_fusion
  94.4 0.9 broadcast_in_dim.37
  95.3 3.5 %all-to-all-start.3 = ((bf16[8,18,1536]{2,1,0:T(8,128)(2,1)}), bf16[8,18,1536]{2,1,0:T(8,128)(2,1)S(1)}, u32[]{:S(2)}, u32[]{:S(2)}) async-start(bf16[8,18,1536]{2,1,0:T(8,128)(2,1)} %bitcast.9), calls=%async_computation.3 | async-start | bytes 1179648 | tf_op jit(solution)/shard_map/all_to_all | solution.py:110
  98.9 0.1 reshape.138
  99.0 14.8 %all-to-all-done.3 = bf16[8,18,1536]{2,1,0:T(8,128)(2,1)S(1)} async-done(((bf16[8,18,1536]{2,1,0:T(8,128)(2,1)}), bf16[8,18,1536]{2,1,0:T(8,128)(2,1)S(1)}, u32[]{:S(2)}, u32[]{:S(2)}) %all-to-all-start.3) | async-done | bytes 442400 | tf_op jit(solution)/shard_map/all_to_all | solution.py:110
  113.9 8.9 %select_reduce_fusion = f32[144,16]{0,1:T(8,128)S(1)} fusion(bf16[144,1536,1]{1,0,2:T(8,128)(2,1)S(1)} %reshape.150, bf16[16,256,1536]{2,1,0:T(8,128)(2,1)} %bitcast.51, s32[144,16]{0,1:T(8,128)S(1)} %broadcast_subtract_fusion), kind=kOutput, calls=%fused_computation.6 | convolution fusion | flops 1813706496 | bytes 13043712 | tf_op jit(solution)/shard_map/dot_general | solution.py:42
  122.9 10.3 %psum.15 = bf16[144,16]{0,1:T(8,128)(2,1)S(1)} all-reduce(f32[144,16]{0,1:T(8,128)S(1)} %select_reduce_fusion), channel_id=1, replica_groups=mesh['expert'=8,'chan'=4] {'chan'}, use_global_device_ids=true, to_apply=%region_5.6 | all-reduce | flops 2304 | bytes 13824 | tf_op jit(solution)/shard_map/psum | solution.py:45
  133.2 1.2 fusion.10
  134.6 10.8 %fusion.34 = f32[1536,4096]{1,0:T(8,128)} fusion(bf16[144,1536]{1,0:T(8,128)(2,1)S(1)} %reshape.138, bf16[144,4096]{1,0:T(8,128)(2,1)S(1)} %bitcast.48), kind=kOutput, calls=%fused_computation.48 | convolution fusion | flops 1811939328 | bytes 26787840 | tf_op jit(solution)/shard_map/dot_general | solution.py:50
  145.6 10.8 %fusion.35 = f32[4096,1536]{1,0:T(8,128)} fusion(bf16[144,4096]{1,0:T(8,128)(2,1)S(1)} %bitcast.47, bf16[144,1536]{1,0:T(8,128)(2,1)S(1)} %reshape.142), kind=kOutput, calls=%fused_computation.49 | convolution fusion | flops 1811939328 | bytes 26787840 | tf_op jit(solution)/shard_map/dot_general | solution.py:47
  (25 shorter events, 1.5 us)
Async XLA Ops:
  4.0 13.9 %all-to-all-start = ((s32[8,1,576]{2,1,0:T(1,128)}), s32[8,1,576]{2,1,0:T(1,128)S(1)}, u32[]{:S(2)}, u32[]{:S(2)}) async-start(s32[8,1,576]{2,1,0:T(1,128)} %reshape.154), calls=%async_computation | async-start | bytes 40960 | tf_op jit(solution)/shard_map/all_to_all | solution.py:88
  18.7 24.2 %all-to-all-start.1 = ((bf16[8,18,1536]{2,1,0:T(8,128)(2,1)}), bf16[8,18,1536]{2,1,0:T(8,128)(2,1)S(1)}, u32[]{:S(2)}, u32[]{:S(2)}) async-start(bf16[8,18,1536]{2,1,0:T(8,128)(2,1)} %bitcast.2), calls=%async_computation.1 | async-start | bytes 1179648 | tf_op jit(solution)/shard_map/all_to_all | solution.py:87
  71.7 22.1 %copy-start = (bf16[32,1536]{1,0:T(8,128)(2,1)S(1)}, bf16[32,1536]{1,0:T(8,128)(2,1)}, u32[]{:S(2)}) copy-start(bf16[32,1536]{1,0:T(8,128)(2,1)} %param.5) | copy-start | bytes 294916
  94.2 28.6 %copy-start.1 = (bf16[32,1536]{1,0:T(8,128)(2,1)}, bf16[32,1536]{1,0:T(8,128)(2,1)S(1)}, u32[]{:S(2)}) copy-start(bf16[32,1536]{1,0:T(8,128)(2,1)S(1)} %fusion.6) | copy-start | bytes 294916
  95.3 18.5 %all-to-all-start.3 = ((bf16[8,18,1536]{2,1,0:T(8,128)(2,1)}), bf16[8,18,1536]{2,1,0:T(8,128)(2,1)S(1)}, u32[]{:S(2)}, u32[]{:S(2)}) async-start(bf16[8,18,1536]{2,1,0:T(8,128)(2,1)} %bitcast.9), calls=%async_computation.3 | async-start | bytes 1179648 | tf_op jit(solution)/shard_map/all_to_all | solution.py:110

commit v2 on v0

v2 whole, which is shorter than its diff:
```python
import functools

import jax
import jax.numpy as jnp
from jax import lax
from jax.experimental import pallas as pl
from jax.experimental.pallas import tpu as pltpu
from jax.sharding import PartitionSpec as P

LAT = 8192
EXPERTS = 4
TOPK = 32
CAP = 18
STRIDE = LAT // TOPK
LANES = 128
F32 = jnp.float32
BF16 = jnp.bfloat16
PARAMS = pltpu.CompilerParams(vmem_limit_bytes=40 * 1024 * 1024)


def up(value, step):
    return -(-value // step) * step


def iota(shape, dim):
    return lax.broadcasted_iota(jnp.int32, shape, dim)


def dot(left, right, dims):
    return lax.dot_general(left, right, (dims, ((), ())), preferred_element_type=F32)


NN = ((1,), (0,))
NT = ((1,), (1,))
TN = ((0,), (0,))


def put_slots(message_ref, device, table, first):
    for piece in range(table.shape[1] // LANES):
        message_ref[device, pl.ds((first + piece) * CAP, CAP), :] = table[
            :, piece * LANES : (piece + 1) * LANES
        ]


def take_slots(message_ref, device, flat_ref, row):
    for piece in range(flat_ref.shape[1] // LANES):
        flat_ref[pl.ds(row, CAP), piece * LANES : (piece + 1) * LANES] = message_ref[
            device, pl.ds(piece * CAP, CAP), :
        ]


def clear(flat_ref, first):
    if first < flat_ref.shape[0]:
        shape = (flat_ref.shape[0] - first, flat_ref.shape[1])
        flat_ref[first:, :] = jnp.zeros(shape, BF16)


def dispatch_kernel(group, blocks, picks_ref, ids_ref, rows_ref, slots_ref, message_ref):
    rows = rows_ref.shape[0]
    shape = (EXPERTS * CAP, rows)
    number = iota(shape, 0)
    expert = sum((number >= CAP * e).astype(jnp.int32) for e in range(1, EXPERTS))
    place = number - expert * CAP
    hits = [picks_ref[j : j + 1, :] == expert for j in range(2)]
    member = (hits[0] | hits[1]).astype(BF16)
    earlier = (iota((rows, rows), 0) < iota((rows, rows), 1)).astype(BF16)
    slot = dot(member, earlier, NN)
    here = slot == place.astype(F32)
    chosen = [(hit & here).astype(BF16) for hit in hits]
    slots = chosen[0] + chosen[1]
    slots_ref[...] = slots
    sent = dot(slots, rows_ref[...], NN).astype(BF16)
    first = iota((rows, TOPK), 1) * STRIDE
    sent_places = sum(
        dot(chosen[j], (ids_ref[:, j, :] - first + 1).astype(BF16), NN) for j in range(2)
    )
    sent_places = (sent_places - 1.0).astype(BF16)
    pieces = rows_ref.shape[1] // LANES
    empty = jnp.full((CAP, LANES), -1.0, BF16)
    for device in range(message_ref.shape[0]):
        e, low = device // group, device % group * blocks
        part = slice(e * CAP, (e + 1) * CAP)
        put_slots(message_ref, device, sent[part], 0)
        message_ref[device, pl.ds(pieces * CAP, CAP), :] = empty
        message_ref[device, pl.ds(pieces * CAP, CAP), 0:blocks] = sent_places[
            part, low : low + blocks
        ]


def encode_kernel(
    devices, message_ref, enc_ref, rows_t_ref, places_ref, places_t_ref, live_ref, flat, wide, live
):
    blocks = enc_ref.shape[1] // STRIDE
    slots = devices * CAP
    pieces = flat.shape[1] // LANES
    step = pl.program_id(0)

    @pl.when(step == 0)
    def _():
        wide[...] = jnp.full(wide.shape, -1.0, F32)
        live[...] = jnp.zeros(live.shape, F32)
        for device in range(devices):
            take_slots(message_ref, device, flat, device * CAP)
            wide[pl.ds(device * CAP, CAP), :] = message_ref[
                device, pl.ds(pieces * CAP, CAP), :
            ].astype(F32)
        places_ref[...] = wide[...]

    partial = dot(flat[0:slots, :], enc_ref[...], NN)
    lane = iota((slots, STRIDE), 1).astype(F32)
    column = iota((slots, LANES), 1)
    for block in range(blocks):
        index = step * blocks + block
        place = jnp.sum(
            jnp.where(column == index, wide[0:slots, :], 0.0), axis=1, keepdims=True
        )
        part = partial[:, block * STRIDE : (block + 1) * STRIDE]
        value = jnp.sum(jnp.where(place == lane, part, 0.0), axis=1, keepdims=True)
        live[0:slots, :] = jnp.where(column == index, value, live[0:slots, :])

    @pl.when(step == pl.num_programs(0) - 1)
    def _():
        count = live_ref.shape[0]
        live_ref[...] = live[...].T[0:count, :]
        places_t_ref[...] = wide[...].T[0:count, :]
        clear(flat, slots)
        rows_t_ref[...] = flat[...].T


def turned(values):
    count, width = values.shape
    full = jnp.concatenate([values, jnp.zeros((LANES - count, width), F32)], axis=0)
    return full.T


def recon_kernel(devices, parts_ref, places_ref, dec_ref, message_ref, live_ref, live, total):
    blocks = dec_ref.shape[0] // STRIDE
    slots = devices * CAP
    step = pl.program_id(0)

    @pl.when(step == 0)
    def _():
        values = jnp.sum(parts_ref[...], axis=0)
        live_ref[...] = values
        live[...] = turned(values)
        total[...] = jnp.zeros(total.shape, F32)

    lane = iota((slots, STRIDE), 1).astype(F32)
    column = iota((slots, LANES), 1)
    pieces = []
    for block in range(blocks):
        here = column == step * blocks + block
        place = jnp.sum(jnp.where(here, places_ref[0:slots, :], 0.0), axis=1, keepdims=True)
        value = jnp.sum(jnp.where(here, live[0:slots, :], 0.0), axis=1, keepdims=True)
        pieces.append(jnp.where(place == lane, value, 0.0).astype(BF16))
    total[...] += dot(jnp.concatenate(pieces, axis=1), dec_ref[...], NN)

    @pl.when(step == pl.num_programs(0) - 1)
    def _():
        for device in range(devices):
            table = total[pl.ds(device * CAP, CAP), :].astype(BF16)
            put_slots(message_ref, device, table, 0)


def error_kernel(group, message_ref, slots_ref, rows_ref, error_ref, sent_ref, back):
    slots = slots_ref[...]
    recon = jnp.zeros(rows_ref.shape, F32)
    for member in range(group):
        for e in range(EXPERTS):
            take_slots(message_ref, e * group + member, back, e * CAP)
        recon = recon + dot(slots, back[...], TN)
    error = (recon - rows_ref[...].astype(F32)).astype(BF16)
    error_ref[...] = error
    sent = dot(slots, error, NN).astype(BF16)
    for device in range(sent_ref.shape[0]):
        e = device // group
        put_slots(sent_ref, device, sent[e * CAP : (e + 1) * CAP], 0)


def latent_kernel(devices, message_ref, places_t_ref, dec_ref, flat_ref, grad_ref):
    blocks = dec_ref.shape[0] // STRIDE
    slots = devices * CAP
    step = pl.program_id(0)

    @pl.when(step == 0)
    def _():
        for device in range(devices):
            take_slots(message_ref, device, flat_ref, device * CAP)
        clear(flat_ref, slots)

    partial = dot(dec_ref[...], flat_ref[...], NT)
    width = flat_ref.shape[0]
    row = iota((STRIDE, width), 0).astype(F32)
    for block in range(blocks):
        index = step * blocks + block
        part = partial[block * STRIDE : (block + 1) * STRIDE, :]
        here = places_t_ref[pl.ds(index, 1), :] == row
        grad_ref[pl.ds(index, 1), :] = jnp.sum(
            jnp.where(here, part, 0.0), axis=0, keepdims=True
        )


def dec_grad_kernel(places_t_ref, live_ref, flat_ref, out_ref):
    blocks = out_ref.shape[0] // STRIDE
    step = pl.program_id(0)
    row = iota((STRIDE, flat_ref.shape[0]), 0).astype(F32)
    for block in range(blocks):
        index = step * blocks + block
        here = places_t_ref[pl.ds(index, 1), :] == row
        activation = jnp.where(here, live_ref[pl.ds(index, 1), :], 0.0).astype(BF16)
        out_ref[block * STRIDE : (block + 1) * STRIDE, :] = dot(activation, flat_ref[...], NN)


def enc_grad_kernel(rows_t_ref, places_ref, mine_ref, other_ref, out_ref, live):
    blocks = out_ref.shape[1] // STRIDE
    step = pl.program_id(0)

    @pl.when(step == 0)
    def _():
        live[...] = turned(mine_ref[...] + other_ref[...])

    shape = (places_ref.shape[0], STRIDE)
    lane = iota(shape, 1).astype(F32)
    column = iota(places_ref.shape, 1)
    for block in range(blocks):
        here = column == step * blocks + block
        place = jnp.sum(jnp.where(here, places_ref[...], 0.0), axis=1, keepdims=True)
        value = jnp.sum(jnp.where(here, live[...], 0.0), axis=1, keepdims=True)
        pre_grad = jnp.where(place == lane, value, 0.0).astype(BF16)
        out_ref[:, block * STRIDE : (block + 1) * STRIDE] = dot(rows_t_ref[...], pre_grad, NN)


def whole(shape):
    return pl.BlockSpec(shape, lambda *_: (0,) * len(shape))


def struct(shape, dtype):
    return jax.ShapeDtypeStruct(shape, dtype)


def cost(flops, moved):
    return pl.CostEstimate(flops=flops, bytes_accessed=moved, transcendentals=0)


def per_device(rows_in, expert_picks, latent_ids, enc_weight, dec_weight):
    row_count, chan = rows_in.shape
    devices = lax.axis_size("expert")
    chans = lax.axis_size("chan")
    group = devices // EXPERTS
    lat = enc_weight.shape[1]
    blocks = lat // STRIDE
    slots = devices * CAP
    padded = up(slots, LANES)
    pieces = chan // LANES
    deep = up((pieces + 1) * CAP, 16)
    thin = up(pieces * CAP, 16)
    tile = min(lat, 2 * STRIDE)
    steps = lat // tile
    matmul = 2 * slots * chan * lat

    def exchange(message):
        return lax.all_to_all(message, "expert", split_axis=0, concat_axis=0, tiled=True)

    slot_table, message = pl.pallas_call(
        functools.partial(dispatch_kernel, group, blocks),
        out_shape=(
            struct((EXPERTS * CAP, row_count), BF16),
            struct((devices, deep, LANES), BF16),
        ),
        compiler_params=PARAMS,
        name="dispatch",
    )(expert_picks.T, latent_ids, rows_in)
    message = exchange(message)
    rows_t, places, places_t, live = pl.pallas_call(
        functools.partial(encode_kernel, devices),
        grid=(steps,),
        in_specs=[whole(message.shape), pl.BlockSpec((chan, tile), lambda i: (0, i))],
        out_specs=(
            whole((chan, padded)),
            whole((padded, LANES)),
            whole((blocks, padded)),
            whole((blocks, padded)),
        ),
        out_shape=(
            struct((chan, padded), BF16),
            struct((padded, LANES), F32),
            struct((blocks, padded), F32),
            struct((blocks, padded), F32),
        ),
        scratch_shapes=[
            pltpu.VMEM((padded, chan), BF16),
            pltpu.VMEM((padded, LANES), F32),
            pltpu.VMEM((padded, LANES), F32),
        ],
        compiler_params=PARAMS,
        cost_estimate=cost(matmul, 2 * chan * lat),
        name="encode",
    )(message, enc_weight)
    parts = lax.all_gather(live, "chan")
    message, live = pl.pallas_call(
        functools.partial(recon_kernel, devices),
        grid=(steps,),
        in_specs=[
            whole(parts.shape),
            whole(places.shape),
            pl.BlockSpec((tile, chan), lambda i: (i, 0)),
        ],
        out_specs=(whole((devices, thin, LANES)), whole((blocks, padded))),
        out_shape=(struct((devices, thin, LANES), BF16), struct((blocks, padded), F32)),
        scratch_shapes=[pltpu.VMEM((padded, LANES), F32), pltpu.VMEM((slots, chan), F32)],
        compiler_params=PARAMS,
        cost_estimate=cost(matmul, 2 * chan * lat),
        name="recon",
    )(parts, places, dec_weight)
    message = exchange(message)
    recon_error, message = pl.pallas_call(
        functools.partial(error_kernel, group),
        out_shape=(struct(rows_in.shape, BF16), struct((devices, thin, LANES), BF16)),
        scratch_shapes=[pltpu.VMEM((EXPERTS * CAP, chan), BF16)],
        compiler_params=PARAMS,
        name="error",
    )(message, slot_table, rows_in)
    message = exchange(message)
    flat_errors, grad = pl.pallas_call(
        functools.partial(latent_kernel, devices),
        grid=(steps,),
        in_specs=[
            whole(message.shape),
            whole(places_t.shape),
            pl.BlockSpec((tile, chan), lambda i: (i, 0)),
        ],
        out_specs=(whole((padded, chan)), whole((blocks, padded))),
        out_shape=(struct((padded, chan), BF16), struct((blocks, padded), F32)),
        compiler_params=PARAMS,
        cost_estimate=cost(matmul, 2 * chan * lat),
        name="latent",
    )(message, places_t, dec_weight)
    swap = [[(i, i ^ bit) for i in range(chans)] for bit in (1, 2)]
    grad = grad + lax.ppermute(grad, "chan", swap[0])
    other = lax.ppermute(grad, "chan", swap[1])
    dec_grad = pl.pallas_call(
        dec_grad_kernel,
        grid=(steps,),
        in_specs=[whole(places_t.shape), whole(live.shape), whole(flat_errors.shape)],
        out_specs=pl.BlockSpec((tile, chan), lambda i: (i, 0)),
        out_shape=struct(dec_weight.shape, F32),
        compiler_params=PARAMS,
        cost_estimate=cost(matmul, 4 * chan * lat),
        name="dec_grad",
    )(places_t, live, flat_errors)
    enc_grad = pl.pallas_call(
        enc_grad_kernel,
        grid=(steps,),
        in_specs=[
            whole(rows_t.shape),
            whole(places.shape),
            whole(grad.shape),
            whole(other.shape),
        ],
        out_specs=pl.BlockSpec((chan, tile), lambda i: (0, i)),
        out_shape=struct(enc_weight.shape, F32),
        scratch_shapes=[pltpu.VMEM((padded, LANES), F32)],
        compiler_params=PARAMS,
        cost_estimate=cost(matmul, 4 * chan * lat),
        name="enc_grad",
    )(rows_t, places, grad, other)
    return (recon_error, enc_grad, dec_grad)


def solution(mesh):
    placed = (
        P("expert", "chan"),
        P("expert", None),
        P("expert", None, None),
        P("chan", "expert"),
        P("expert", "chan"),
    )
    return jax.shard_map(
        per_device,
        mesh=mesh,
        in_specs=placed,
        out_specs=(P("expert", "chan"), P("chan", "expert"), P("expert", "chan")),
        check_vma=False,
    )
```

time: 209 us -> 117 us (0.56)
  matrix products: 49.6 us -> 0 us
  waiting for transfers between devices: 41.4 us -> 1.17 us
  Pallas kernels: 0 us -> 36.7 us
  blocking collectives: 85 us -> 59.8 us
  between operations: 14.3 us -> 0.68 us
  local copies, waits for them, and re-layouts: 5.84 us -> 16.1 us
  starting transfers between devices: 10.9 us -> 1.58 us
    dot_general x11 -> x0, matrix products: 49.6 us -> none  [the longest x1 12 us: gradients(): lax.dot_general(flat_rows, pre_grad, (((0,), (0,)), ((), ())), preferred_...]
    psum x1 -> x0, blocking collectives: 45.4 us -> none  [encode(): preact = lax.psum(partial_pre, 'chan')]
    pallas_call x0 -> x7, Pallas kernels: none -> 36.7 us  [the longest x1 10.8 us: per_device(): pl.pallas_call(enc_grad_kernel, grid=(steps,), in_specs=[whole(rows_t.sha...]
    psum x1 -> x0, waiting for transfers between devices: 25.4 us -> none  [gradients(): lax.psum(partial_grad.astype(jnp.bfloat16), 'chan').astype(jnp.float32)]
    all_to_all x2 -> x0, waiting for transfers between devices: 16 us -> none  [the longest x1 10.5 us: per_device(): lax.all_to_all(fan_out(sent_rows), 'expert', split_axis=0, concat_axis=0,...]
    all_to_all x2 -> x3, blocking collectives: 39.5 us -> 54.6 us  [exchange(): lax.all_to_all(message, 'expert', split_axis=0, concat_axis=0, tiled=True)]
    unnamed x10 -> x14, local copies, waits for them, and re-layouts: 3.47 us -> 16.1 us
    all_to_all x2 -> x0, starting transfers between devices: 10.8 us -> none  [the longest x1 7.28 us: per_device(): lax.all_to_all(fan_out(sent_ids), 'expert', split_axis=0, concat_axis=0,...]
  transfers between devices with their start and end apart: 3 -> 2, of which waited for: 3 -> 1; matrix products, arithmetic and copies ran while one was open for 8% -> 0% of each run, Pallas kernels for 0% -> 9%
where the time goes in v2:
time: 117 us; the launch traced here: 116 us
  blocking collectives  59.8 us (51%)
  Pallas kernels  36.7 us (31%)
  local copies, waits for them, and re-layouts  16.1 us (14%)
  starting transfers between devices  1.58 us (1%)
  waiting for transfers between devices  1.17 us (1%)
    all_to_all x3, blocking collectives, exchange(): lax.all_to_all(message, 'expert', split_axis=0, concat_axis=0, tiled=True)  54.6 us
    unnamed x14, local copies, waits for them, and re-layouts  16.1 us
    pallas_call x1, Pallas kernels, per_device(): pl.pallas_call(enc_grad_kernel, grid=(steps,), in_specs=[whole(rows_t.sha...  10.8 us
    pallas_call x1, Pallas kernels, per_device(): pl.pallas_call(dec_grad_kernel, grid=(steps,), in_specs=[whole(places_t.s...  9.99 us
    pallas_call x1, Pallas kernels, per_device(): pl.pallas_call(functools.partial(encode_kernel, devices), grid=(steps,),...  5.52 us
    all_gather x1, blocking collectives, per_device(): parts = lax.all_gather(live, 'chan')  5.24 us
    pallas_call x1, Pallas kernels, per_device(): pl.pallas_call(functools.partial(latent_kernel, devices), grid=(steps,),...  5.14 us
    pallas_call x1, Pallas kernels, per_device(): pl.pallas_call(functools.partial(recon_kernel, devices), grid=(steps,), i...  3.87 us
  transfers between devices with their start and end apart: 2, of which 1 were waited for; matrix products, arithmetic and copies ran while one was open for 0% of the time, Pallas kernels for 9%

profile of v2, /device:TPU:0, one launch (start us, length us, event | category | flops | bytes accessed | tf_op | source)
XLA Modules:
  0.0 116.0 jit_solution(9136419822116526177)
XLA Ops:
  0.6 0.0 copy-start.3
  0.6 0.9 copy-done.3
  1.5 0.0 copy-start.5
  1.5 0.8 copy-done.5
  2.3 0.0 copy-start.6
  2.3 0.7 copy-done.6
  3.0 0.0 copy-start.4
  3.0 0.4 dispatch.1
  3.4 20.9 %all_to_all.15.message_ref = bf16[8,240,128]{2,1,0:T(8,128)(2,1)S(1)} all-to-all(bf16[8,240,128]{2,1,0:T(8,128)(2,1)S(1)} %get-tuple-element.15), channel_id=1, replica_groups=mesh['expert'=8,'chan'=4] {'expert'}, dimensions={0} | all-to-all | bytes 983040 | tf_op jit(solution)/shard_map/all_to_all | solution.py:262
  24.3 0.0 copy-start.2
  24.3 4.6 %copy-done.2 = bf16[1536,4096]{1,0:T(8,128)(2,1)S(1)} copy-done((bf16[1536,4096]{1,0:T(8,128)(2,1)S(1)}, bf16[1536,4096]{1,0:T(8,128)(2,1)}, u32[]{:S(2)}) %copy-start.2) | copy-done | bytes 12582936
  28.9 5.5 %encode.1 = (bf16[1536,256]{1,0:T(8,128)(2,1)S(1)}, f32[256,128]{1,0:T(8,128)S(1)}, f32[16,256]{1,0:T(8,128)S(1)}, f32[16,256]{1,0:T(8,128)S(1)}) custom-call(bf16[8,240,128]{2,1,0:T(8,128)(2,1)S(1)} %all_to_all.15.message_ref, bf16[1536,4096]{1,0:T(8,128)(2,1)S(1)} %copy-done.2), custom_call_target="tpu_custom_call" | custom-call | flops 1811939328 | bytes 12582912 | tf_op jit(solution)/shard_map/encode/pallas_call | solution.py:274
  34.4 5.2 %all-gather = f32[64,256]{1,0:T(8,128)S(1)} all-gather(f32[16,256]{1,0:T(8,128)S(1)} %get-tuple-element.16), channel_id=2, replica_groups=mesh['expert'=8,'chan'=4] {'chan'}, dimensions={0}, use_global_device_ids=true | all-gather | bytes 81920 | tf_op jit(solution)/shard_map/all_gather | solution.py:299
  39.6 0.0 copy-start
  39.6 4.6 %copy-done = bf16[4096,1536]{1,0:T(8,128)(2,1)S(1)} copy-done((bf16[4096,1536]{1,0:T(8,128)(2,1)S(1)}, bf16[4096,1536]{1,0:T(8,128)(2,1)}, u32[]{:S(2)}) %copy-start) | copy-done | bytes 12582936
  44.2 3.9 %recon.1 = (bf16[8,224,128]{2,1,0:T(8,128)(2,1)S(1)}, f32[16,256]{1,0:T(8,128)S(1)}) custom-call(f32[4,16,256]{2,1,0:T(8,128)S(1)} %bitcast.2, f32[256,128]{1,0:T(8,128)S(1)} %get-tuple-element.17.places_ref, bf16[4096,1536]{1,0:T(8,128)(2,1)S(1)} %copy-done), custom_call_target="tpu_custom_call" | custom-call | flops 1811939328 | bytes 12582912 | tf_op jit(solution)/shard_map/recon/pallas_call | solution.py:300
  48.1 17.1 %all_to_all.16.message_ref = bf16[8,224,128]{2,1,0:T(8,128)(2,1)S(1)} all-to-all(bf16[8,224,128]{2,1,0:T(8,128)(2,1)S(1)} %get-tuple-element.18), channel_id=1, replica_groups=mesh['expert'=8,'chan'=4] {'expert'}, dimensions={0} | all-to-all | bytes 917504 | tf_op jit(solution)/shard_map/all_to_all | solution.py:262
  65.2 0.0 copy-done.4
  65.2 1.0 error.1
  66.2 16.6 %all_to_all.17.message_ref = bf16[8,224,128]{2,1,0:T(8,128)(2,1)S(1)} all-to-all(bf16[8,224,128]{2,1,0:T(8,128)(2,1)S(1)} %get-tuple-element.22), channel_id=1, replica_groups=mesh['expert'=8,'chan'=4] {'expert'}, dimensions={0} | all-to-all | bytes 917504 | tf_op jit(solution)/shard_map/all_to_all | solution.py:262
  82.8 0.0 copy-start.1
  82.8 4.6 %copy-done.1 = bf16[4096,1536]{1,0:T(8,128)(2,1)S(1)} copy-done((bf16[4096,1536]{1,0:T(8,128)(2,1)S(1)}, bf16[4096,1536]{1,0:T(8,128)(2,1)}, u32[]{:S(2)}) %copy-start.1) | copy-done | bytes 12582936
  87.4 5.1 %latent.1 = (bf16[256,1536]{1,0:T(8,128)(2,1)S(1)}, f32[16,256]{1,0:T(8,128)S(1)}) custom-call(bf16[8,224,128]{2,1,0:T(8,128)(2,1)S(1)} %all_to_all.17.message_ref, f32[16,256]{1,0:T(8,128)S(1)} %get-tuple-element.23.places_t_ref, bf16[4096,1536]{1,0:T(8,128)(2,1)S(1)} %copy-done.1), custom_call_target="tpu_custom_call" | custom-call | flops 1811939328 | bytes 12582912 | tf_op jit(solution)/shard_map/latent/pallas_call | solution.py:324
  92.5 0.1 collective-permute-start
  92.6 1.2 %collective-permute-done = f32[16,256]{1,0:T(8,128)S(1)} collective-permute-done((f32[16,256]{1,0:T(8,128)S(1)}, f32[16,256]{1,0:T(8,128)S(1)}, u32[]{:S(2)}, u32[]{:S(2)}) %collective-permute-start) | collective-permute-done | bytes 16416 | tf_op jit(solution)/shard_map/ppermute | solution.py:339
  93.8 1.5 %collective-permute-start.1 = (f32[16,256]{1,0:T(8,128)S(1)}, f32[16,256]{1,0:T(8,128)S(1)}, u32[]{:S(2)}, u32[]{:S(2)}) collective-permute-start(f32[16,256]{1,0:T(8,128)S(1)} %add.3.mine_ref), channel_id=1, source_target_pairs={{0,2},{1,3},{2,0},{3,1},{4,6},{5,7},{6,4},{7,5},{8,10},{9,11},{10,... | collective-permute-start | bytes 49160 | tf_op jit(solution)/shard_map/ppermute | solution.py:340
  95.3 10.0 %dec_grad.1 = f32[4096,1536]{1,0:T(8,128)} custom-call(f32[16,256]{1,0:T(8,128)S(1)} %get-tuple-element.23.places_t_ref, f32[16,256]{1,0:T(8,128)S(1)} %get-tuple-element.25.live_ref, bf16[256,1536]{1,0:T(8,128)(2,1)S(1)} %get-tuple-element.26.flat_ref), custom_call_target="tpu_custom_call" | custom-call | flops 1811939328 | bytes 25165824 | tf_op jit(solution)/shard_map/dec_grad/pallas_call | solution.py:341
  105.3 0.0 collective-permute-done.1.other_ref
  105.3 10.8 %enc_grad.1 = f32[1536,4096]{1,0:T(8,128)} custom-call(bf16[1536,256]{1,0:T(8,128)(2,1)S(1)} %get-tuple-element.21.rows_t_ref, f32[256,128]{1,0:T(8,128)S(1)} %get-tuple-element.17.places_ref, f32[16,256]{1,0:T(8,128)S(1)} %add.3.mine_ref, f32[16,256]{1,0:T(8,128)S(1)} %collective-permute-done.1.other_ref), custom_call_target="tpu_custom_call" | custom-call | flops 1811939328 | bytes 25165824 | tf_op jit(solution)/shard_map/enc_grad/pallas_call | solution.py:351
  (1 shorter events, 0.0 us)
Async XLA Ops:
  0.6 0.9 copy-start.3
  1.5 0.8 copy-start.5
  2.3 0.7 copy-start.6
  3.0 62.2 %copy-start.4 = (bf16[32,1536]{1,0:T(8,128)(2,1)S(1)}, bf16[32,1536]{1,0:T(8,128)(2,1)}, u32[]{:S(2)}) copy-start(bf16[32,1536]{1,0:T(8,128)(2,1)} %rows_ref.3) | copy-start | bytes 294916
  24.3 4.6 %copy-start.2 = (bf16[1536,4096]{1,0:T(8,128)(2,1)S(1)}, bf16[1536,4096]{1,0:T(8,128)(2,1)}, u32[]{:S(2)}) copy-start(bf16[1536,4096]{1,0:T(8,128)(2,1)} %enc_ref.1) | copy-start | bytes 37748740
  39.6 4.6 %copy-start = (bf16[4096,1536]{1,0:T(8,128)(2,1)S(1)}, bf16[4096,1536]{1,0:T(8,128)(2,1)}, u32[]{:S(2)}) copy-start(bf16[4096,1536]{1,0:T(8,128)(2,1)} %dec_ref.3) | copy-start | bytes 37748740
  82.8 4.6 %copy-start.1 = (bf16[4096,1536]{1,0:T(8,128)(2,1)S(1)}, bf16[4096,1536]{1,0:T(8,128)(2,1)}, u32[]{:S(2)}) copy-start(bf16[4096,1536]{1,0:T(8,128)(2,1)} %dec_ref.3) | copy-start | bytes 37748740
  92.5 1.2 %collective-permute-start = (f32[16,256]{1,0:T(8,128)S(1)}, f32[16,256]{1,0:T(8,128)S(1)}, u32[]{:S(2)}, u32[]{:S(2)}) collective-permute-start(f32[16,256]{1,0:T(8,128)S(1)} %get-tuple-element.24), channel_id=1, source_target_pairs={{0,1},{1,0},{2,3},{3,2},{4,5},{5,4},{6,7},{7,6},{8,9},{9,8},{10,11... | collective-permute-start | bytes 49160 | tf_op jit(solution)/shard_map/ppermute | solution.py:339
  93.8 11.5 %collective-permute-start.1 = (f32[16,256]{1,0:T(8,128)S(1)}, f32[16,256]{1,0:T(8,128)S(1)}, u32[]{:S(2)}, u32[]{:S(2)}) collective-permute-start(f32[16,256]{1,0:T(8,128)S(1)} %add.3.mine_ref), channel_id=1, source_target_pairs={{0,2},{1,3},{2,0},{3,1},{4,6},{5,7},{6,4},{7,5},{8,10},{9,11},{10,... | collective-permute-start | bytes 49160 | tf_op jit(solution)/shard_map/ppermute | solution.py:340
